TPU v7x, 32 devices: a whole 2x2x4 slice. The times are simulated.
32 devices in a mesh: group: 2 (over x), col: 16 (over z, y, core).
Axes of the slice: x: 2, y: 2, z: 4, core: 2. Of those that a mesh axis runs over, the one named last changes fastest.
Arguments:
- homolog_embedding: bfloat16 [192, 64, 256], P('group', 'col'), parts along dimension 0, may hold values from -6 to 6
- left_factor_matrix: bfloat16 [256, 32], replicated, may hold values from -0.375 to 0.375
- right_factor_matrix: bfloat16 [256, 32], replicated, may hold values from -0.375 to 0.375
- decoder: bfloat16 [1024, 128], replicated, may hold values from -2 to 2
- pair_output_bias: float32 [128], replicated, may hold values from -3 to 3
- pair_output_gradient: bfloat16 [128, 64, 128], P('group', 'col'), parts along dimension 0, may hold values from -6 to 6
Outputs:
- first_operand_gradient: float32 [192, 64, 32], P('group', 'col'), parts along dimension 0
- second_operand_gradient: float32 [192, 64, 32], P('group', 'col'), parts along dimension 0
- alignment_gradient: bfloat16 [192, 64, 256], P('group', 'col'), parts along dimension 0
There are 2 independent parts, one for each index of `group`. A program takes and returns all parts, laid end to end along the dimension named above; an argument that names none is the same for every part. Nothing has to cross between parts.
All inputs are finite; a program needn't handle non-finite values.
Results may differ from a plain program's by a relative error of at most 0.0083.
Values may be sent and summed in bfloat16 or wider, within the bound.
A program may use at most 64 MiB of HBM per device.

v0:
```python
import jax
import jax.numpy as jnp
from jax import lax
from jax.sharding import PartitionSpec as P


def per_device(
    homolog_embedding,
    left_factor_matrix,
    right_factor_matrix,
    decoder,
    pair_output_bias,
    pair_output_gradient,
):
    alignment_row_count, local_residue_start, alignment_channel_width = homolog_embedding.shape
    operand_channel_width = left_factor_matrix.shape[1]
    channels = decoder.shape[1]
    residue_total_count = local_residue_start * lax.axis_size("col")
    reciprocal_rows = 1.0 / alignment_row_count
    block_res = local_residue_start * max(1, 96 // local_residue_start)
    alignment_flattened_rows = homolog_embedding.reshape(
        alignment_row_count * local_residue_start, alignment_channel_width
    )
    first_operand_rows = (
        jnp.dot(alignment_flattened_rows, left_factor_matrix, preferred_element_type=jnp.float32)
        .astype(jnp.bfloat16)
        .reshape(alignment_row_count, local_residue_start * operand_channel_width)
    )
    second_operand_rows = (
        jnp.dot(alignment_flattened_rows, right_factor_matrix, preferred_element_type=jnp.float32)
        .astype(jnp.bfloat16)
        .reshape(alignment_row_count, local_residue_start * operand_channel_width)
    )
    second_operand_local = second_operand_rows.reshape(
        alignment_row_count, local_residue_start, operand_channel_width
    )

    def outer_slopes(slope_rows, rows_by_length, col_span):
        backward = (
            jnp.dot(slope_rows, decoder.T, preferred_element_type=jnp.float32) * reciprocal_rows
        )
        return backward.astype(jnp.bfloat16).reshape(
            rows_by_length, col_span, operand_channel_width, operand_channel_width
        )

    offset_col = jnp.int32(0)
    second_operand_gradient = jnp.zeros(
        (alignment_row_count, local_residue_start, operand_channel_width), jnp.float32
    )
    stored = jnp.zeros((residue_total_count, local_residue_start * channels), jnp.bfloat16)
    left_segment = lax.all_gather(first_operand_rows, "col", axis=1, tiled=True)
    right_segment = lax.all_gather(second_operand_rows, "col", axis=1, tiled=True)
    right_whole = right_segment
    piece_res = left_segment.shape[1] // operand_channel_width
    first_res = offset_col // operand_channel_width
    collected = []
    for split_offset in range(0, piece_res, block_res):
        split_rows_by_length = min(block_res, piece_res - split_offset)
        split_left_block = left_segment[
            :,
            split_offset
            * operand_channel_width : (split_offset + split_rows_by_length)
            * operand_channel_width,
        ].reshape(alignment_row_count, split_rows_by_length, operand_channel_width)
        collected.append((split_rows_by_length, split_left_block, first_res + split_offset))
    for rows_by_length, left_block, first_row in collected:
        products = (
            jnp.einsum(
                "sic,sjd->ijcd",
                left_block,
                second_operand_local,
                preferred_element_type=jnp.float32,
            )
            * reciprocal_rows
        )
        products = products.astype(jnp.bfloat16).reshape(
            rows_by_length * local_residue_start, operand_channel_width * operand_channel_width
        )
        linear = jnp.dot(products, decoder, preferred_element_type=jnp.float32) + pair_output_bias
        upstream = lax.dynamic_slice_in_dim(pair_output_gradient, first_row, rows_by_length, 0)
        upstream = upstream.reshape(rows_by_length * local_residue_start, channels).astype(
            jnp.float32
        )
        accumulate_slope_rows = (upstream * 2.0 * jnp.maximum(linear, 0.0)).astype(jnp.bfloat16)
        stored = lax.dynamic_update_slice_in_dim(
            stored,
            accumulate_slope_rows.reshape(rows_by_length, local_residue_start * channels),
            first_row,
            0,
        )
        accumulate_slopes = outer_slopes(accumulate_slope_rows, rows_by_length, local_residue_start)
        second_operand_gradient = second_operand_gradient + jnp.einsum(
            "ijcd,sic->sjd", accumulate_slopes, left_block, preferred_element_type=jnp.float32
        )
    second_operand_gradient, stored, right_whole = (second_operand_gradient, stored, right_whole)
    received = lax.all_to_all(stored, "col", split_axis=0, concat_axis=1, tiled=True)
    right_all = right_whole.reshape(alignment_row_count, residue_total_count, operand_channel_width)
    col_span = local_residue_start * max(
        max(1, 96 // local_residue_start), lax.axis_size("col") // 8
    )
    first_operand_gradient = jnp.zeros(
        (alignment_row_count, local_residue_start, operand_channel_width), jnp.float32
    )
    for offset in range(0, residue_total_count, col_span):
        width_cols = min(col_span, residue_total_count - offset)
        slope_rows = received[:, offset * channels : (offset + width_cols) * channels].reshape(
            local_residue_start * width_cols, channels
        )
        slopes = outer_slopes(slope_rows, local_residue_start, width_cols)
        first_operand_gradient = first_operand_gradient + jnp.einsum(
            "ijcd,sjd->sic",
            slopes,
            right_all[:, offset : offset + width_cols],
            preferred_element_type=jnp.float32,
        )
    first_operand_gradient_step = first_operand_gradient.astype(jnp.bfloat16).reshape(
        alignment_row_count * local_residue_start, operand_channel_width
    )
    second_operand_gradient_step = second_operand_gradient.astype(jnp.bfloat16).reshape(
        alignment_row_count * local_residue_start, operand_channel_width
    )
    alignment_gradient = jnp.dot(
        first_operand_gradient_step, left_factor_matrix.T, preferred_element_type=jnp.float32
    ) + jnp.dot(
        second_operand_gradient_step, right_factor_matrix.T, preferred_element_type=jnp.float32
    )
    alignment_gradient = alignment_gradient.astype(jnp.bfloat16).reshape(
        alignment_row_count, local_residue_start, alignment_channel_width
    )
    return (first_operand_gradient, second_operand_gradient, alignment_gradient)


def solution(mesh):
    placed = (P("group", "col", None), P(), P(), P(), P(), P("group", "col", None))
    return jax.shard_map(
        per_device,
        mesh=mesh,
        in_specs=placed,
        out_specs=(P("group", "col", None), P("group", "col", None), P("group", "col", None)),
        check_vma=False,
    )
```

profile of v0, /device:TPU:0, one launch (start us, length us, event | category | flops | bytes accessed | tf_op | source)
XLA Modules:
  0.0 74.2 jit_solution(9161705522396213601)
XLA Ops:
  0.6 0.0 copy-start
  0.6 0.0 copy-start.3
  0.7 1.0 %reshape.53 = bf16[384,256]{1,0:T(8,128)(2,1)S(1)} reshape(bf16[96,4,256]{2,1,0:T(4,128)(2,1)} %param.6) | data formatting | bytes 393216 | tf_op jit(solution)/shard_map/reshape | solution.py:21
  1.7 0.9 %convolution_convert_fusion = bf16[384,32]{0,1:T(8,128)(2,1)S(1)} fusion(bf16[384,256]{1,0:T(8,128)(2,1)S(1)} %reshape.53, bf16[256,32]{0,1:T(8,128)(2,1)} %param.7), kind=kOutput, calls=%fused_computation.14 | convolution fusion | flops 6303744 | bytes 237568 | tf_op jit(solution)/shard_map/dot_general | solution.py:25
  2.6 0.1 copy.31
  2.7 0.1 reshape.56
  2.8 24.2 %all_gather.7 = bf16[96,2048]{1,0:T(8,128)(2,1)S(1)} all-gather(bf16[96,128]{1,0:T(8,128)(2,1)S(1)} %reshape.56), channel_id=1, replica_groups=mesh['group'=2,'col'=16] {'col'}, dimensions={1}, use_global_device_ids=true | all-gather | bytes 417792 | tf_op jit(solution)/shard_map/all_gather | solution.py:51
  27.0 0.3 copy.32
  27.3 0.0 copy-done.3
  27.3 0.2 convolution_convert_fusion.1
  27.5 0.1 copy.28
  27.6 1.6 %fusion = bf16[64,4,32,32]{0,3,2,1:T(8,128)(2,1)} fusion(bf16[96,64,32]{0,2,1:T(8,128)(2,1)S(1)} %bitcast.48, bf16[96,4,32,1]{2,1,0,3:T(4,128)(2,1)S(1)} %bitcast.51), kind=kOutput, calls=%fused_computation.1 | convolution fusion | flops 50855936 | bytes 942080 | tf_op jit(solution)/shard_map/sic,sjd->ijcd/dot_general | solution.py:68
  29.3 4.2 %copy.35 = bf16[64,4,32,32]{3,2,1,0:T(8,128)(2,1)S(1)} copy(bf16[64,4,32,32]{0,3,2,1:T(8,128)(2,1)} %fusion) | data formatting | bytes 1048576 | tf_op jit(solution)/shard_map/convert_element_type | solution.py:76
  33.5 0.0 copy-start.4
  33.5 2.2 %reshape.58 = bf16[256,1024]{1,0:T(8,128)(2,1)S(1)} reshape(bf16[64,4,32,32]{3,2,1,0:T(8,128)(2,1)S(1)} %copy.35) | data formatting | bytes 1048576 | tf_op jit(solution)/shard_map/reshape | solution.py:76
  35.7 0.9 %convert_multiply_fusion = f32[64,4,128]{2,1,0:T(4,128)S(1)} fusion(bf16[64,4,128]{2,1,0:T(4,128)(2,1)} %param.11), kind=kLoop, calls=%fused_computation.18 | loop fusion | flops 65536 | bytes 196608 | tf_op jit(solution)/shard_map/mul | solution.py:84
  36.6 0.0 copy-done
  36.6 0.0 copy-done.4
  36.6 0.3 fusion.6
  36.9 0.7 all_to_all.12
  37.6 4.2 %all-to-all-start = ((bf16[16,4,512]{2,1,0:T(4,128)(2,1)}), bf16[16,4,512]{2,1,0:T(4,128)(2,1)}, u32[]{:S(2)}, u32[]{:S(2)}) async-start(bf16[16,4,512]{2,1,0:T(4,128)(2,1)} %all_to_all.12), calls=%async_computation | async-start | bytes 131072 | tf_op jit(solution)/shard_map/all_to_all | solution.py:96
  41.7 0.7 reshape.54
  42.5 0.3 fusion.2
  42.8 0.0 copy-start.1
  42.8 1.6 %reshape.61 = bf16[64,4,32,32]{3,2,1,0:T(8,128)(2,1)S(1)} reshape(bf16[256,1024]{1,0:T(8,128)(2,1)S(1)} %fusion.2) | data formatting | bytes 1048576 | tf_op jit(solution)/shard_map/reshape | solution.py:42
  44.4 1.3 %fusion.11 = (bf16[96,4,32]{0,2,1:T(8,128)(2,1)S(1)}, f32[96,4,32]{0,2,1:T(8,128)}) fusion(bf16[96,64,32,1]{0,2,3,1:T(8,128)(2,1)S(1)} %bitcast.49, bf16[64,4,32,32]{3,2,1,0:T(8,128)(2,1)S(1)} %reshape.61), kind=kOutput, calls=%fused_computation.21 | convolution fusion | flops 50343936 | bytes 991232 | tf_op jit(solution)/shard_map/ijcd,sic->sjd/dot_general | solution.py:92
  45.7 0.0 copy-done.1
  45.7 22.7 %all_gather.6 = bf16[96,2048]{1,0:T(8,128)(2,1)S(1)} all-gather(bf16[96,128]{1,0:T(8,128)(2,1)S(1)} %copy-done.1), channel_id=1, replica_groups=mesh['group'=2,'col'=16] {'col'}, dimensions={1}, use_global_device_ids=true | all-gather | bytes 417792 | tf_op jit(solution)/shard_map/all_gather | solution.py:52
  68.4 0.3 copy.29
  68.7 0.1 copy.41
  68.8 0.0 all-to-all-done
  68.8 0.9 %copy.36 = bf16[4,16,512]{2,1,0:T(8,128)(2,1)S(1)} copy(bf16[4,16,512]{2,0,1:T(4,128)(2,1)} %bitcast.8) | data formatting | bytes 131072 | tf_op jit(solution)/shard_map/all_to_all | solution.py:96
  69.7 0.1 reshape.59
  69.7 0.3 fusion.1
  70.0 0.0 copy-start.2
  70.0 1.6 %reshape.71 = bf16[4,64,32,32]{3,2,1,0:T(8,128)(2,1)S(1)} reshape(bf16[256,1024]{1,0:T(8,128)(2,1)S(1)} %fusion.1) | data formatting | bytes 1048576 | tf_op jit(solution)/shard_map/reshape | solution.py:42
  71.6 1.3 %fusion.10 = (bf16[96,4,32]{0,2,1:T(8,128)(2,1)S(1)}, f32[96,4,32]{0,2,1:T(8,128)}) fusion(bf16[96,64,32,1]{0,2,1,3:T(8,128)(2,1)S(1)} %bitcast.50, bf16[4,64,32,32]{3,2,1,0:T(8,128)(2,1)S(1)} %reshape.71), kind=kOutput, calls=%fused_computation.20 | convolution fusion | flops 50343936 | bytes 991232 | tf_op jit(solution)/shard_map/ijcd,sjd->sic/dot_general | solution.py:110
  73.0 0.1 copy.40
  73.1 0.0 copy-done.2
  73.1 0.2 fusion.12
  73.3 0.2 fusion.3
  73.5 0.7 reshape.64
Async XLA Ops:
  0.6 36.0 %copy-start = (bf16[1024,128]{1,0:T(8,128)(2,1)S(1)}, bf16[1024,128]{1,0:T(8,128)(2,1)}, u32[]{:S(2)}) copy-start(bf16[1024,128]{1,0:T(8,128)(2,1)} %param.9) | copy-start | bytes 786436
  0.6 26.7 %copy-start.3 = (bf16[256,32]{0,1:T(8,128)(2,1)S(1)}, bf16[256,32]{0,1:T(8,128)(2,1)}, u32[]{:S(2)}) copy-start(bf16[256,32]{0,1:T(8,128)(2,1)} %param.8) | copy-start | bytes 49156
  33.5 3.1 %copy-start.4 = (f32[128]{0:T(128)S(1)}, f32[128]{0:T(128)}, u32[]{:S(2)}) copy-start(f32[128]{0:T(128)} %param.10) | copy-start | bytes 1540
  37.6 31.2 %all-to-all-start = ((bf16[16,4,512]{2,1,0:T(4,128)(2,1)}), bf16[16,4,512]{2,1,0:T(4,128)(2,1)}, u32[]{:S(2)}, u32[]{:S(2)}) async-start(bf16[16,4,512]{2,1,0:T(4,128)(2,1)} %all_to_all.12), calls=%async_computation | async-start | bytes 131072 | tf_op jit(solution)/shard_map/all_to_all | solution.py:96
  42.8 3.0 %copy-start.1 = (bf16[96,128]{1,0:T(8,128)(2,1)S(1)}, bf16[96,128]{1,0:T(8,128)(2,1)}, u32[]{:S(2)}) copy-start(bf16[96,128]{1,0:T(8,128)(2,1)} %reshape.54) | copy-start | bytes 73732
  70.0 3.1 %copy-start.2 = (bf16[256,32]{0,1:T(8,128)(2,1)S(1)}, bf16[256,32]{0,1:T(8,128)(2,1)}, u32[]{:S(2)}) copy-start(bf16[256,32]{0,1:T(8,128)(2,1)} %param.7) | copy-start | bytes 49156
where the time goes:
time: 74.6 us; the launch traced here: 74.2 us
  blocking collectives  46.9 us (63%)
  local copies, waits for them, and re-layouts  14.9 us (20%)
  matrix products  6.57 us (9%)
  starting transfers between devices  4.16 us (6%)
  other arithmetic  0.87 us (1%)
  between operations  0.86 us (1%)
    all_gather x1, blocking collectives, per_device(): left_segment = lax.all_gather(first_operand_rows, 'col', axis=1, tiled=True)  24.2 us
    all_gather x1, blocking collectives, per_device(): lax.all_gather(second_operand_rows, 'col', axis=1, tiled=True)  22.7 us
    convert_element_type x1, local copies, waits for them, and re-layouts, per_device(): products.astype(jnp.bfloat16)  4.19 us
    all_to_all x1, starting transfers between devices, per_device(): lax.all_to_all(stored, 'col', split_axis=0, concat_axis=1, tiled=True)  4.16 us
    reshape x2, local copies, waits for them, and re-layouts, outer_slopes(): backward.astype(jnp.bfloat16)  3.16 us
    reshape x1, local copies, waits for them, and re-layouts, per_device(): products.astype(jnp.bfloat16)  2.23 us
    dot_general x1, matrix products, per_device(): jnp.einsum('sic,sjd->ijcd', left_block, second_operand_local, preferred_e...  1.63 us
    all_to_all x2, local copies, waits for them, and re-layouts, per_device(): lax.all_to_all(stored, 'col', split_axis=0, concat_axis=1, tiled=True)  1.52 us
  transfers between devices with their start and end apart: 1, of which 0 were waited for; matrix products, arithmetic and copies ran while one was open for 6% of the time, Pallas kernels for 0%

commit v1 on v0

--- a/solution.py
+++ b/solution.py
@@ -48,7 +48,12 @@
         (alignment_row_count, local_residue_start, operand_channel_width), jnp.float32
     )
     stored = jnp.zeros((residue_total_count, local_residue_start * channels), jnp.bfloat16)
-    left_segment = lax.all_gather(first_operand_rows, "col", axis=1, tiled=True)
+    ring = [first_operand_rows]
+    for hop in range(15):
+        ring.append(lax.ppermute(ring[-1], "col", [(dev, (dev + 1) % 16) for dev in range(16)]))
+    left_segment = jnp.roll(
+        jnp.concatenate(ring[::-1], axis=1), (lax.axis_index("col") + 1) * ring[0].shape[1], axis=1
+    )
     right_segment = lax.all_gather(second_operand_rows, "col", axis=1, tiled=True)
     right_whole = right_segment
     piece_res = left_segment.shape[1] // operand_channel_width

time: 74.6 us -> 136 us (1.82)
  waiting for transfers between devices: 0.01 us -> 87.2 us
  blocking collectives: 46.9 us -> 19.1 us
    ppermute x0 -> x15, waiting for transfers between devices: none -> 81.8 us  [per_device(): lax.ppermute(ring[-1], 'col', [(dev, (dev + 1) % 16) for dev in range(16)])]
    all_gather x1 -> x0, blocking collectives: 24.2 us -> none  [per_device(): left_segment = lax.all_gather(first_operand_rows, 'col', axis=1, tiled=True)]
    all_to_all x1, waiting for transfers between devices: 0.01 us -> 5.43 us  [per_device(): lax.all_to_all(stored, 'col', split_axis=0, concat_axis=1, tiled=True)]
    all_gather x1, blocking collectives: 22.7 us -> 19.1 us  [per_device(): lax.all_gather(second_operand_rows, 'col', axis=1, tiled=True)]
  transfers between devices with their start and end apart: 1 -> 16, of which waited for: 0 -> 15; matrix products, arithmetic and copies ran while one was open for 6% -> 3% of each run, Pallas kernels for 0% -> 0%
where the time goes in v1:
time: 136 us
  waiting for transfers between devices  87.2 us (64%)
  blocking collectives  19.1 us (14%)
  local copies, waits for them, and re-layouts  15.4 us (11%)
  matrix products  7.32 us (5%)
  starting transfers between devices  4.74 us (3%)
    ppermute x15, waiting for transfers between devices, per_device(): lax.ppermute(ring[-1], 'col', [(dev, (dev + 1) % 16) for dev in range(16)])  81.8 us
    all_gather x1, blocking collectives, per_device(): lax.all_gather(second_operand_rows, 'col', axis=1, tiled=True)  19.1 us
    all_to_all x1, waiting for transfers between devices, per_device(): lax.all_to_all(stored, 'col', split_axis=0, concat_axis=1, tiled=True)  5.43 us
    convert_element_type x1, local copies, waits for them, and re-layouts, per_device(): products.astype(jnp.bfloat16)  4.19 us
    all_to_all x1, starting transfers between devices, per_device(): lax.all_to_all(stored, 'col', split_axis=0, concat_axis=1, tiled=True)  4.16 us
    reshape x2, local copies, waits for them, and re-layouts, outer_slopes(): backward.astype(jnp.bfloat16)  3.15 us
  transfers between devices with their start and end apart: 16, of which 15 were waited for; matrix products, arithmetic and copies ran while one was open for 3% of the time, Pallas kernels for 0%

profile of v1, /device:TPU:0, one launch (start us, length us, event | category | flops | bytes accessed | tf_op | source)
XLA Modules:
  0.0 135.6 jit_solution(7585390603305414176)
XLA Ops:
  0.6 0.0 copy-start
  0.6 1.0 reshape.53
  1.7 0.9 convolution_convert_fusion
  2.6 0.1 copy.31
  2.7 0.1 reshape.56
  2.8 0.5 collective-permute-start
  3.4 6.5 %collective-permute-done = bf16[96,128]{1,0:T(8,128)(2,1)S(1)} collective-permute-done((bf16[96,128]{1,0:T(8,128)(2,1)S(1)}, bf16[96,128]{1,0:T(8,128)(2,1)S(1)}, u32[]{:S(2)}, u32[]{:S(2)}) %collective-permute-start) | collective-permute-done | bytes 24608 | tf_op jit(solution)/shard_map/ppermute | solution.py:53
  9.9 0.0 collective-permute-start.1
  9.9 5.9 %collective-permute-done.1 = bf16[96,128]{1,0:T(8,128)(2,1)S(1)} collective-permute-done((bf16[96,128]{1,0:T(8,128)(2,1)S(1)}, bf16[96,128]{1,0:T(8,128)(2,1)S(1)}, u32[]{:S(2)}, u32[]{:S(2)}) %collective-permute-start.1) | collective-permute-done | bytes 24608 | tf_op jit(solution)/shard_map/ppermute | solution.py:53
  15.8 0.0 collective-permute-start.2
  15.8 5.9 %collective-permute-done.2 = bf16[96,128]{1,0:T(8,128)(2,1)S(1)} collective-permute-done((bf16[96,128]{1,0:T(8,128)(2,1)S(1)}, bf16[96,128]{1,0:T(8,128)(2,1)S(1)}, u32[]{:S(2)}, u32[]{:S(2)}) %collective-permute-start.2) | collective-permute-done | bytes 24608 | tf_op jit(solution)/shard_map/ppermute | solution.py:53
  21.8 0.0 collective-permute-start.3
  21.8 5.9 %collective-permute-done.3 = bf16[96,128]{1,0:T(8,128)(2,1)S(1)} collective-permute-done((bf16[96,128]{1,0:T(8,128)(2,1)S(1)}, bf16[96,128]{1,0:T(8,128)(2,1)S(1)}, u32[]{:S(2)}, u32[]{:S(2)}) %collective-permute-start.3) | collective-permute-done | bytes 24608 | tf_op jit(solution)/shard_map/ppermute | solution.py:53
  27.7 0.0 collective-permute-start.4
  27.7 5.9 %collective-permute-done.4 = bf16[96,128]{1,0:T(8,128)(2,1)S(1)} collective-permute-done((bf16[96,128]{1,0:T(8,128)(2,1)S(1)}, bf16[96,128]{1,0:T(8,128)(2,1)S(1)}, u32[]{:S(2)}, u32[]{:S(2)}) %collective-permute-start.4) | collective-permute-done | bytes 24608 | tf_op jit(solution)/shard_map/ppermute | solution.py:53
  33.7 0.0 collective-permute-start.5
  33.7 5.9 %collective-permute-done.5 = bf16[96,128]{1,0:T(8,128)(2,1)S(1)} collective-permute-done((bf16[96,128]{1,0:T(8,128)(2,1)S(1)}, bf16[96,128]{1,0:T(8,128)(2,1)S(1)}, u32[]{:S(2)}, u32[]{:S(2)}) %collective-permute-start.5) | collective-permute-done | bytes 24608 | tf_op jit(solution)/shard_map/ppermute | solution.py:53
  39.6 0.0 collective-permute-start.6
  39.6 5.9 %collective-permute-done.6 = bf16[96,128]{1,0:T(8,128)(2,1)S(1)} collective-permute-done((bf16[96,128]{1,0:T(8,128)(2,1)S(1)}, bf16[96,128]{1,0:T(8,128)(2,1)S(1)}, u32[]{:S(2)}, u32[]{:S(2)}) %collective-permute-start.6) | collective-permute-done | bytes 24608 | tf_op jit(solution)/shard_map/ppermute | solution.py:53
  45.6 0.0 collective-permute-start.7
  45.6 5.9 %collective-permute-done.7 = bf16[96,128]{1,0:T(8,128)(2,1)S(1)} collective-permute-done((bf16[96,128]{1,0:T(8,128)(2,1)S(1)}, bf16[96,128]{1,0:T(8,128)(2,1)S(1)}, u32[]{:S(2)}, u32[]{:S(2)}) %collective-permute-start.7) | collective-permute-done | bytes 24608 | tf_op jit(solution)/shard_map/ppermute | solution.py:53
  51.5 0.0 collective-permute-start.8
  51.5 5.9 %collective-permute-done.8 = bf16[96,128]{1,0:T(8,128)(2,1)S(1)} collective-permute-done((bf16[96,128]{1,0:T(8,128)(2,1)S(1)}, bf16[96,128]{1,0:T(8,128)(2,1)S(1)}, u32[]{:S(2)}, u32[]{:S(2)}) %collective-permute-start.8) | collective-permute-done | bytes 24608 | tf_op jit(solution)/shard_map/ppermute | solution.py:53
  57.5 5.9 %collective-permute-done.9 = bf16[96,128]{1,0:T(8,128)(2,1)S(1)} collective-permute-done((bf16[96,128]{1,0:T(8,128)(2,1)S(1)}, bf16[96,128]{1,0:T(8,128)(2,1)S(1)}, u32[]{:S(2)}, u32[]{:S(2)}) %collective-permute-start.9) | collective-permute-done | bytes 24608 | tf_op jit(solution)/shard_map/ppermute | solution.py:53
  63.4 0.0 collective-permute-start.10
  63.4 5.9 %collective-permute-done.10 = bf16[96,128]{1,0:T(8,128)(2,1)S(1)} collective-permute-done((bf16[96,128]{1,0:T(8,128)(2,1)S(1)}, bf16[96,128]{1,0:T(8,128)(2,1)S(1)}, u32[]{:S(2)}, u32[]{:S(2)}) %collective-permute-start.10) | collective-permute-done | bytes 24608 | tf_op jit(solution)/shard_map/ppermute | solution.py:53
  69.4 0.0 collective-permute-start.11
  69.4 5.9 %collective-permute-done.11 = bf16[96,128]{1,0:T(8,128)(2,1)S(1)} collective-permute-done((bf16[96,128]{1,0:T(8,128)(2,1)S(1)}, bf16[96,128]{1,0:T(8,128)(2,1)S(1)}, u32[]{:S(2)}, u32[]{:S(2)}) %collective-permute-start.11) | collective-permute-done | bytes 24608 | tf_op jit(solution)/shard_map/ppermute | solution.py:53
  75.3 0.9 convolution_convert_fusion.1
  76.2 5.1 %collective-permute-done.12 = bf16[96,128]{1,0:T(8,128)(2,1)S(1)} collective-permute-done((bf16[96,128]{1,0:T(8,128)(2,1)S(1)}, bf16[96,128]{1,0:T(8,128)(2,1)S(1)}, u32[]{:S(2)}, u32[]{:S(2)}) %collective-permute-start.12) | collective-permute-done | bytes 24608 | tf_op jit(solution)/shard_map/ppermute | solution.py:53
  81.3 0.0 collective-permute-start.13
  81.3 0.9 convert_multiply_fusion
  82.1 0.1 copy.28
  82.3 0.1 reshape.54
  82.4 4.8 %collective-permute-done.13 = bf16[96,128]{1,0:T(8,128)(2,1)S(1)} collective-permute-done((bf16[96,128]{1,0:T(8,128)(2,1)S(1)}, bf16[96,128]{1,0:T(8,128)(2,1)S(1)}, u32[]{:S(2)}, u32[]{:S(2)}) %collective-permute-start.13) | collective-permute-done | bytes 24608 | tf_op jit(solution)/shard_map/ppermute | solution.py:53
  87.2 0.0 collective-permute-start.14
  87.2 19.1 %all_gather.3 = bf16[96,2048]{1,0:T(8,128)(2,1)S(1)} all-gather(bf16[96,128]{1,0:T(8,128)(2,1)S(1)} %reshape.54), channel_id=1, replica_groups=mesh['group'=2,'col'=16] {'col'}, dimensions={1}, use_global_device_ids=true | all-gather | bytes 417792 | tf_op jit(solution)/shard_map/all_gather | solution.py:57
  106.3 1.0 copy.29
  107.3 0.0 collective-permute-done.14
  107.8 0.3 copy.32
  108.1 1.7 %fusion = bf16[64,4,32,32]{0,3,2,1:T(8,128)(2,1)} fusion(bf16[96,64,32]{0,2,1:T(8,128)(2,1)S(1)} %bitcast.48, bf16[96,4,32,1]{2,1,0,3:T(4,128)(2,1)S(1)} %bitcast.51), kind=kOutput, calls=%fused_computation.1 | convolution fusion | flops 50855936 | bytes 942080 | tf_op jit(solution)/shard_map/sic,sjd->ijcd/dot_general | solution.py:73
  109.8 4.2 %copy.35 = bf16[64,4,32,32]{3,2,1,0:T(8,128)(2,1)S(1)} copy(bf16[64,4,32,32]{0,3,2,1:T(8,128)(2,1)} %fusion) | data formatting | bytes 1048576 | tf_op jit(solution)/shard_map/convert_element_type | solution.py:81
  114.0 0.0 copy-start.4
  114.0 2.2 %reshape.58 = bf16[256,1024]{1,0:T(8,128)(2,1)S(1)} reshape(bf16[64,4,32,32]{3,2,1,0:T(8,128)(2,1)S(1)} %copy.35) | data formatting | bytes 1048576 | tf_op jit(solution)/shard_map/reshape | solution.py:81
  116.2 0.3 fusion.6
  116.5 0.3 fusion.2
  116.8 0.7 all_to_all.12
  117.5 1.6 %reshape.61 = bf16[64,4,32,32]{3,2,1,0:T(8,128)(2,1)S(1)} reshape(bf16[256,1024]{1,0:T(8,128)(2,1)S(1)} %fusion.2) | data formatting | bytes 1048576 | tf_op jit(solution)/shard_map/reshape | solution.py:42
  119.1 4.2 %all-to-all-start = ((bf16[16,4,512]{2,1,0:T(4,128)(2,1)}), bf16[16,4,512]{2,1,0:T(4,128)(2,1)}, u32[]{:S(2)}, u32[]{:S(2)}) async-start(bf16[16,4,512]{2,1,0:T(4,128)(2,1)} %all_to_all.12), calls=%async_computation | async-start | bytes 131072 | tf_op jit(solution)/shard_map/all_to_all | solution.py:101
  123.3 1.3 fusion.11
  124.6 0.1 copy.41
  124.7 5.4 %all-to-all-done = bf16[16,4,512]{2,1,0:T(4,128)(2,1)} async-done(((bf16[16,4,512]{2,1,0:T(4,128)(2,1)}), bf16[16,4,512]{2,1,0:T(4,128)(2,1)}, u32[]{:S(2)}, u32[]{:S(2)}) %all-to-all-start) | async-done | bytes 65568 | tf_op jit(solution)/shard_map/all_to_all | solution.py:101
  130.2 0.9 copy.36
  131.0 0.1 reshape.59
  131.1 0.3 fusion.1
  131.4 0.0 copy-start.2
  131.4 1.6 %reshape.71 = bf16[4,64,32,32]{3,2,1,0:T(8,128)(2,1)S(1)} reshape(bf16[256,1024]{1,0:T(8,128)(2,1)S(1)} %fusion.1) | data formatting | bytes 1048576 | tf_op jit(solution)/shard_map/reshape | solution.py:42
  133.0 0.0 copy-start.3
  133.0 1.3 fusion.10
  134.3 0.1 copy.40
  134.5 0.2 fusion.12
  134.6 0.0 copy-done.3
  134.7 0.2 fusion.3
  134.8 0.7 reshape.64
  (40 shorter events, 0.4 us)
Async XLA Ops:
  0.6 115.6 %copy-start = (bf16[1024,128]{1,0:T(8,128)(2,1)S(1)}, bf16[1024,128]{1,0:T(8,128)(2,1)}, u32[]{:S(2)}) copy-start(bf16[1024,128]{1,0:T(8,128)(2,1)} %param.9) | copy-start | bytes 786436
  2.8 7.0 %collective-permute-start = (bf16[96,128]{1,0:T(8,128)(2,1)S(1)}, bf16[96,128]{1,0:T(8,128)(2,1)S(1)}, u32[]{:S(2)}, u32[]{:S(2)}) collective-permute-start(bf16[96,128]{1,0:T(8,128)(2,1)S(1)} %reshape.56), channel_id=1, source_target_pairs={{0,1},{1,2},{2,3},{3,4},{4,5},{5,6},{6,7},{7,8},{8,9},{9,10},{10,1... | collective-permute-start | bytes 73736 | tf_op jit(solution)/shard_map/ppermute | solution.py:53
  9.9 5.9 %collective-permute-start.1 = (bf16[96,128]{1,0:T(8,128)(2,1)S(1)}, bf16[96,128]{1,0:T(8,128)(2,1)S(1)}, u32[]{:S(2)}, u32[]{:S(2)}) collective-permute-start(bf16[96,128]{1,0:T(8,128)(2,1)S(1)} %collective-permute-done), channel_id=1, source_target_pairs={{0,1},{1,2},{2,3},{3,4},{4,5},{5,6},{6,7},{7,8},{8,9},{9,10},{10,1... | collective-permute-start | bytes 73736 | tf_op jit(solution)/shard_map/ppermute | solution.py:53
  15.8 5.9 %collective-permute-start.2 = (bf16[96,128]{1,0:T(8,128)(2,1)S(1)}, bf16[96,128]{1,0:T(8,128)(2,1)S(1)}, u32[]{:S(2)}, u32[]{:S(2)}) collective-permute-start(bf16[96,128]{1,0:T(8,128)(2,1)S(1)} %collective-permute-done.1), channel_id=1, source_target_pairs={{0,1},{1,2},{2,3},{3,4},{4,5},{5,6},{6,7},{7,8},{8,9},{9,10},{10,1... | collective-permute-start | bytes 73736 | tf_op jit(solution)/shard_map/ppermute | solution.py:53
  21.8 5.9 %collective-permute-start.3 = (bf16[96,128]{1,0:T(8,128)(2,1)S(1)}, bf16[96,128]{1,0:T(8,128)(2,1)S(1)}, u32[]{:S(2)}, u32[]{:S(2)}) collective-permute-start(bf16[96,128]{1,0:T(8,128)(2,1)S(1)} %collective-permute-done.2), channel_id=1, source_target_pairs={{0,1},{1,2},{2,3},{3,4},{4,5},{5,6},{6,7},{7,8},{8,9},{9,10},{10,1... | collective-permute-start | bytes 73736 | tf_op jit(solution)/shard_map/ppermute | solution.py:53
  27.7 5.9 %collective-permute-start.4 = (bf16[96,128]{1,0:T(8,128)(2,1)S(1)}, bf16[96,128]{1,0:T(8,128)(2,1)S(1)}, u32[]{:S(2)}, u32[]{:S(2)}) collective-permute-start(bf16[96,128]{1,0:T(8,128)(2,1)S(1)} %collective-permute-done.3), channel_id=1, source_target_pairs={{0,1},{1,2},{2,3},{3,4},{4,5},{5,6},{6,7},{7,8},{8,9},{9,10},{10,1... | collective-permute-start | bytes 73736 | tf_op jit(solution)/shard_map/ppermute | solution.py:53
  33.7 5.9 %collective-permute-start.5 = (bf16[96,128]{1,0:T(8,128)(2,1)S(1)}, bf16[96,128]{1,0:T(8,128)(2,1)S(1)}, u32[]{:S(2)}, u32[]{:S(2)}) collective-permute-start(bf16[96,128]{1,0:T(8,128)(2,1)S(1)} %collective-permute-done.4), channel_id=1, source_target_pairs={{0,1},{1,2},{2,3},{3,4},{4,5},{5,6},{6,7},{7,8},{8,9},{9,10},{10,1... | collective-permute-start | bytes 73736 | tf_op jit(solution)/shard_map/ppermute | solution.py:53
  39.6 5.9 %collective-permute-start.6 = (bf16[96,128]{1,0:T(8,128)(2,1)S(1)}, bf16[96,128]{1,0:T(8,128)(2,1)S(1)}, u32[]{:S(2)}, u32[]{:S(2)}) collective-permute-start(bf16[96,128]{1,0:T(8,128)(2,1)S(1)} %collective-permute-done.5), channel_id=1, source_target_pairs={{0,1},{1,2},{2,3},{3,4},{4,5},{5,6},{6,7},{7,8},{8,9},{9,10},{10,1... | collective-permute-start | bytes 73736 | tf_op jit(solution)/shard_map/ppermute | solution.py:53
  45.6 5.9 %collective-permute-start.7 = (bf16[96,128]{1,0:T(8,128)(2,1)S(1)}, bf16[96,128]{1,0:T(8,128)(2,1)S(1)}, u32[]{:S(2)}, u32[]{:S(2)}) collective-permute-start(bf16[96,128]{1,0:T(8,128)(2,1)S(1)} %collective-permute-done.6), channel_id=1, source_target_pairs={{0,1},{1,2},{2,3},{3,4},{4,5},{5,6},{6,7},{7,8},{8,9},{9,10},{10,1... | collective-permute-start | bytes 73736 | tf_op jit(solution)/shard_map/ppermute | solution.py:53
  51.5 5.9 %collective-permute-start.8 = (bf16[96,128]{1,0:T(8,128)(2,1)S(1)}, bf16[96,128]{1,0:T(8,128)(2,1)S(1)}, u32[]{:S(2)}, u32[]{:S(2)}) collective-permute-start(bf16[96,128]{1,0:T(8,128)(2,1)S(1)} %collective-permute-done.7), channel_id=1, source_target_pairs={{0,1},{1,2},{2,3},{3,4},{4,5},{5,6},{6,7},{7,8},{8,9},{9,10},{10,1... | collective-permute-start | bytes 73736 | tf_op jit(solution)/shard_map/ppermute | solution.py:53
  57.5 5.9 %collective-permute-start.9 = (bf16[96,128]{1,0:T(8,128)(2,1)S(1)}, bf16[96,128]{1,0:T(8,128)(2,1)S(1)}, u32[]{:S(2)}, u32[]{:S(2)}) collective-permute-start(bf16[96,128]{1,0:T(8,128)(2,1)S(1)} %collective-permute-done.8), channel_id=1, source_target_pairs={{0,1},{1,2},{2,3},{3,4},{4,5},{5,6},{6,7},{7,8},{8,9},{9,10},{10,1... | collective-permute-start | bytes 73736 | tf_op jit(solution)/shard_map/ppermute | solution.py:53
  63.4 5.9 %collective-permute-start.10 = (bf16[96,128]{1,0:T(8,128)(2,1)S(1)}, bf16[96,128]{1,0:T(8,128)(2,1)S(1)}, u32[]{:S(2)}, u32[]{:S(2)}) collective-permute-start(bf16[96,128]{1,0:T(8,128)(2,1)S(1)} %collective-permute-done.9), channel_id=1, source_target_pairs={{0,1},{1,2},{2,3},{3,4},{4,5},{5,6},{6,7},{7,8},{8,9},{9,10},{10,1... | collective-permute-start | bytes 73736 | tf_op jit(solution)/shard_map/ppermute | solution.py:53
  69.4 5.9 %collective-permute-start.11 = (bf16[96,128]{1,0:T(8,128)(2,1)S(1)}, bf16[96,128]{1,0:T(8,128)(2,1)S(1)}, u32[]{:S(2)}, u32[]{:S(2)}) collective-permute-start(bf16[96,128]{1,0:T(8,128)(2,1)S(1)} %collective-permute-done.10), channel_id=1, source_target_pairs={{0,1},{1,2},{2,3},{3,4},{4,5},{5,6},{6,7},{7,8},{8,9},{9,10},{10,1... | collective-permute-start | bytes 73736 | tf_op jit(solution)/shard_map/ppermute | solution.py:53
  75.3 5.9 %collective-permute-start.12 = (bf16[96,128]{1,0:T(8,128)(2,1)S(1)}, bf16[96,128]{1,0:T(8,128)(2,1)S(1)}, u32[]{:S(2)}, u32[]{:S(2)}) collective-permute-start(bf16[96,128]{1,0:T(8,128)(2,1)S(1)} %collective-permute-done.11), channel_id=1, source_target_pairs={{0,1},{1,2},{2,3},{3,4},{4,5},{5,6},{6,7},{7,8},{8,9},{9,10},{10,1... | collective-permute-start | bytes 73736 | tf_op jit(solution)/shard_map/ppermute | solution.py:53
  81.3 5.9 %collective-permute-start.13 = (bf16[96,128]{1,0:T(8,128)(2,1)S(1)}, bf16[96,128]{1,0:T(8,128)(2,1)S(1)}, u32[]{:S(2)}, u32[]{:S(2)}) collective-permute-start(bf16[96,128]{1,0:T(8,128)(2,1)S(1)} %collective-permute-done.12), channel_id=1, source_target_pairs={{0,1},{1,2},{2,3},{3,4},{4,5},{5,6},{6,7},{7,8},{8,9},{9,10},{10,1... | collective-permute-start | bytes 73736 | tf_op jit(solution)/shard_map/ppermute | solution.py:53
  87.2 20.1 %collective-permute-start.14 = (bf16[96,128]{1,0:T(8,128)(2,1)S(1)}, bf16[96,128]{1,0:T(8,128)(2,1)S(1)}, u32[]{:S(2)}, u32[]{:S(2)}) collective-permute-start(bf16[96,128]{1,0:T(8,128)(2,1)S(1)} %collective-permute-done.13), channel_id=1, source_target_pairs={{0,1},{1,2},{2,3},{3,4},{4,5},{5,6},{6,7},{7,8},{8,9},{9,10},{10,1... | collective-permute-start | bytes 73736 | tf_op jit(solution)/shard_map/ppermute | solution.py:53
  114.0 2.3 %copy-start.4 = (f32[128]{0:T(128)S(1)}, f32[128]{0:T(128)}, u32[]{:S(2)}) copy-start(f32[128]{0:T(128)} %param.10) | copy-start | bytes 1540
  119.1 11.1 %all-to-all-start = ((bf16[16,4,512]{2,1,0:T(4,128)(2,1)}), bf16[16,4,512]{2,1,0:T(4,128)(2,1)}, u32[]{:S(2)}, u32[]{:S(2)}) async-start(bf16[16,4,512]{2,1,0:T(4,128)(2,1)} %all_to_all.12), calls=%async_computation | async-start | bytes 131072 | tf_op jit(solution)/shard_map/all_to_all | solution.py:101
  124.6 8.4 %copy-start.1 = (bf16[96,2048]{0,1:T(8,128)(2,1)S(1)}, bf16[96,2048]{0,1:T(8,128)(2,1)}, u32[]{:S(2)}) copy-start(bf16[96,2048]{0,1:T(8,128)(2,1)} %copy.29) | copy-start | bytes 1179652
  131.4 3.1 %copy-start.2 = (bf16[256,32]{0,1:T(8,128)(2,1)S(1)}, bf16[256,32]{0,1:T(8,128)(2,1)}, u32[]{:S(2)}) copy-start(bf16[256,32]{0,1:T(8,128)(2,1)} %param.7) | copy-start | bytes 49156
  133.0 1.7 %copy-start.3 = (bf16[256,32]{0,1:T(8,128)(2,1)S(1)}, bf16[256,32]{0,1:T(8,128)(2,1)}, u32[]{:S(2)}) copy-start(bf16[256,32]{0,1:T(8,128)(2,1)} %param.8) | copy-start | bytes 49156
